TPU v7x, 256 devices: a whole 4x4x8 slice. The times are simulated.
256 devices in a mesh: blk: 32 (over y_hi, z, core), rep: 8 (over x, y_lo).
Axes of the slice: x: 4, y: 4 (y_hi: 2, y_lo: 2; y = y_hi * 2 + y_lo), z: 8, core: 2. Of those that a mesh axis runs over, the one named last changes fastest.
Arguments:
- features: float32 [32768, 128], P('blk'), may hold values from -6 to 6
- factors: float32 [32768, 128], P('blk'), may hold values from -2.4 to 2.4
Outputs:
- grads: float32 [32768, 128], P(('blk', 'rep'))
All inputs are finite; a program needn't handle non-finite values.
Results may differ from a plain program's by a relative error of at most 0.00018.
Values sent between devices are 32-bit elements; how exact they have to be, the bound alone decides.
A program may use at most 128 MiB of HBM per device.

v0:
```python
import jax
import jax.numpy as jnp
from jax import lax
from jax.sharding import PartitionSpec as P


def pair_terms(own_feat, own_fac, part_feat, part_fac):
    hi = lax.Precision.HIGHEST
    width = own_feat.shape[1]
    rank = own_fac.shape[1] // 2
    cross = jnp.dot(own_feat, part_feat.T, precision=hi)
    own_sq = jnp.sum(own_feat * own_feat, axis=1)
    part_sq = jnp.sum(part_feat * part_feat, axis=1)
    kernel = jnp.exp(-(own_sq[:, None] + part_sq[None, :] - 2.0 * cross) / (2.0 * width))
    coupling = jnp.dot(own_fac[:, :rank], part_fac[:, rank:].T, precision=hi)
    coupling = coupling + jnp.dot(own_fac[:, rank:], part_fac[:, :rank].T, precision=hi)
    weight = coupling * kernel
    own_term = jnp.sum(weight, axis=1)[:, None] * own_feat - jnp.dot(
        weight, part_feat, precision=hi
    )
    return (weight, -own_term / width)


def body(features, factors):
    count = features.shape[0]
    replicas = lax.axis_size("rep")
    share = count // replicas
    first = lax.axis_index("rep") * share
    slice_feat = lax.dynamic_slice_in_dim(features, first, share, 0)
    slice_fac = lax.dynamic_slice_in_dim(factors, first, share, 0)
    weight, own_term = pair_terms(
        features,
        factors,
        lax.all_gather(slice_feat, "blk", axis=0, tiled=True),
        lax.all_gather(slice_fac, "blk", axis=0, tiled=True),
    )
    summed = lax.psum_scatter(own_term, "rep", scatter_dimension=0, tiled=True)
    return summed


def solution(mesh):
    placed = (P("blk", None), P("blk", None))
    return jax.shard_map(
        body, mesh=mesh, in_specs=placed, out_specs=P(("blk", "rep"), None), check_vma=False
    )
```

profile of v0, /device:TPU:32, one launch (start us, length us, event | category | flops | bytes accessed | tf_op | source)
XLA Modules:
  0.0 273.3 jit_solution(17942812913476998213)
XLA Ops:
  6.5 0.0 copy-start.3
  6.5 0.0 all-gather.3.cloned.1.call-start
  6.5 1.5 constant_dynamic-slice_fusion.1
  8.1 0.0 all-gather.3.cloned.1.call-update
  8.1 0.0 all-gather.5.cloned.1.call-start
  8.2 1.5 constant_dynamic-slice_fusion
  9.6 0.0 all-gather.5.cloned.1.call-update
  9.7 0.0 reduce-scatter.2.cloned.1.call-start
  9.7 1.2 multiply_reduce_fusion.1
  11.0 0.0 copy-start.2
  11.0 80.9 %all-gather.3.cloned.1.call-done = f32[4096,128]{1,0:T(8,128)} async-done(((f32[128,128]{1,0:T(8,128)}), f32[4096,128]{1,0:T(8,128)}) %all-gather.3.cloned.1.call-update) | async-done | bytes 2097168 | tf_op jit(solution)/shard_map/all_gather | solution.py:35
  91.8 0.0 copy-start.1
  91.8 17.7 %fusion.4 = f32[4096,1024]{1,0:T(8,128)} fusion(f32[4096,128]{1,0:T(8,128)} %all-gather.3.cloned.1.call-done, f32[1024,128]{1,0:T(8,128)} %param.3), kind=kOutput, calls=%fused_computation.5 | convolution fusion | flops 3221225472 | bytes 19398656 | tf_op jit(solution)/shard_map/dot_general | solution.py:16
  109.5 0.0 copy-done.3
  109.5 0.0 copy-done.1
  109.5 16.1 %fusion.6 = f32[4096,1024]{1,0:T(8,128)} fusion(f32[4096,128]{1,0:T(8,128)S(1)} %copy-done.1, f32[1024,128]{1,0:T(8,128)S(1)} %copy-done.3), kind=kOutput, calls=%fused_computation.7 | convolution fusion | flops 3221225472 | bytes 19398656 | tf_op jit(solution)/shard_map/dot_general | solution.py:15
  125.6 45.3 %all-gather.5.cloned.1.call-done = f32[4096,128]{1,0:T(8,128)} async-done(((f32[128,128]{1,0:T(8,128)}), f32[4096,128]{1,0:T(8,128)}) %all-gather.5.cloned.1.call-update) | async-done | bytes 2097168 | tf_op jit(solution)/shard_map/all_gather | solution.py:34
  171.0 2.2 multiply_reduce_fusion
  173.2 0.0 copy-done.2
  173.2 0.0 copy-start
  173.2 25.9 %fusion.12 = (f32[1024]{0:T(1024)S(1)}, f32[1024,4096]{0,1:T(8,128)}) fusion(f32[4096,128]{1,0:T(8,128)} %all-gather.5.cloned.1.call-done, f32[1024,128]{1,0:T(8,128)S(1)} %copy-done.2, f32[4096]{0:T(1024)S(1)} %multiply_reduce_fusion, f32[1024]{0:T(1024)S(1)} %multiply_reduce_fusion.1, f32[4096,1024]{1,0:T(8,128)} %fusion.6, f32[4096,1024]{1,0:T(8,128)} %fusion.4), kind=kOutput, calls=%fused_computation.18 | convolution fusion | flops 6476004352 | bytes 52977664 | tf_op jit(solution)/shard_map/dot_general | solution.py:11
  199.1 0.0 copy-done
  199.1 29.5 %fusion.9 = f32[1024,128]{1,0:T(8,128)} fusion(f32[1024,4096]{0,1:T(8,128)} %get-tuple-element.6, f32[4096,128]{1,0:T(8,128)S(1)} %copy-done, f32[1024,128]{1,0:T(8,128)S(1)} %copy-done.2, f32[1024]{0:T(1024)S(1)} %get-tuple-element.5), kind=kOutput, calls=%fused_computation.12 | convolution fusion | flops 6442975232 | bytes 19927040 | tf_op jit(solution)/shard_map/dot_general | solution.py:18
  228.6 0.0 reduce-scatter.2.cloned.1.call-update
  228.6 38.1 %reduce-scatter.2.cloned.1.call-done = f32[128,128]{1,0:T(8,128)} async-done(((f32[1024,128]{1,0:T(8,128)}), f32[128,128]{1,0:T(8,128)}) %reduce-scatter.2.cloned.1.call-update) | async-done | bytes 65552 | tf_op jit(solution)/shard_map/reduce_scatter | solution.py:37
Async XLA Ops:
  6.5 103.0 %copy-start.3 = (f32[1024,128]{1,0:T(8,128)S(1)}, f32[1024,128]{1,0:T(8,128)}, u32[]{:S(2)}) copy-start(f32[1024,128]{1,0:T(8,128)} %param.3) | copy-start | bytes 1572868
  6.5 85.3 %all-gather.3.cloned.1.call-start = ((), (), s32[]{:S(2)}) async-start(), calls=%async_computation.1 | async-start | bytes 2162688 | tf_op jit(solution)/shard_map/all_gather | solution.py:35
  8.1 162.9 %all-gather.5.cloned.1.call-start = ((), (), s32[]{:S(2)}) async-start(), calls=%async_computation.2 | async-start | bytes 2162688 | tf_op jit(solution)/shard_map/all_gather | solution.py:34
  9.7 257.1 %reduce-scatter.2.cloned.1.call-start = ((), (), s32[]{:S(2)}) async-start(), calls=%async_computation.3 | async-start | bytes 589824 | tf_op jit(solution)/shard_map/reduce_scatter | solution.py:37
  11.0 162.2 %copy-start.2 = (f32[1024,128]{1,0:T(8,128)S(1)}, f32[1024,128]{1,0:T(8,128)}, u32[]{:S(2)}) copy-start(f32[1024,128]{1,0:T(8,128)} %param.2) | copy-start | bytes 1572868
  91.8 17.7 %copy-start.1 = (f32[4096,128]{1,0:T(8,128)S(1)}, f32[4096,128]{1,0:T(8,128)}, u32[]{:S(2)}) copy-start(f32[4096,128]{1,0:T(8,128)} %all-gather.3.cloned.1.call-done) | copy-start | bytes 6291460
  173.2 25.9 %copy-start = (f32[4096,128]{1,0:T(8,128)S(1)}, f32[4096,128]{1,0:T(8,128)}, u32[]{:S(2)}) copy-start(f32[4096,128]{1,0:T(8,128)} %all-gather.5.cloned.1.call-done) | copy-start | bytes 6291460
Sparse Core Ops, SparseCore 0:
  10.1 81.6 all-gather.2
  94.6 76.3 all-gather.4
  228.7 37.9 reduce-scatter.1
where the time goes:
time: 273 us
  waiting for transfers between devices  164 us (60%)
  matrix products  89.2 us (33%)
  between operations  13.2 us (5%)
  other arithmetic  3.45 us (1%)
  local copies, waits for them, and re-layouts  3.04 us (1%)
    all_gather x1, waiting for transfers between devices, body(): lax.all_gather(slice_fac, 'blk', axis=0, tiled=True)  80.9 us
    all_gather x1, waiting for transfers between devices, body(): lax.all_gather(slice_feat, 'blk', axis=0, tiled=True)  45.3 us
    reduce_scatter x1, waiting for transfers between devices, body(): summed = lax.psum_scatter(own_term, 'rep', scatter_dimension=0, tiled=True)  38.1 us
    dot_general x1, matrix products, pair_terms(): jnp.dot(weight, part_feat, precision=hi)  29.5 us
    dot_general x1, matrix products, pair_terms(): cross = jnp.dot(own_feat, part_feat.T, precision=hi)  25.9 us
    dot_general x1, matrix products, pair_terms(): jnp.dot(own_fac[:, rank:], part_fac[:, :rank].T, precision=hi)  17.7 us
    dot_general x1, matrix products, pair_terms(): coupling = jnp.dot(own_fac[:, :rank], part_fac[:, rank:].T, precision=hi)  16.1 us
  transfers between devices with their start and end apart: 3, of which 3 were waited for; matrix products, arithmetic and copies ran while one was open for 13% of the time, Pallas kernels for 0%

commit v1 on v0

--- a/solution.py
+++ b/solution.py
@@ -2,6 +2,13 @@
 import jax.numpy as jnp
 from jax import lax
 from jax.sharding import PartitionSpec as P
+
+
+def swapped_in(x, name, dim):
+    n_dev = lax.axis_size(name)
+    shards = jnp.stack([x for _ in range(n_dev)])
+    shards = lax.all_to_all(shards, name, split_axis=0, concat_axis=0)
+    return jnp.concatenate(shards, axis=dim)
 
 
 def pair_terms(own_feat, own_fac, part_feat, part_fac):
@@ -32,7 +39,7 @@
         features,
         factors,
         lax.all_gather(slice_feat, "blk", axis=0, tiled=True),
-        lax.all_gather(slice_fac, "blk", axis=0, tiled=True),
+        swapped_in(slice_fac, "blk", 0),
     )
     summed = lax.psum_scatter(own_term, "rep", scatter_dimension=0, tiled=True)
     return summed

time: 273 us -> 213 us (0.78)
  waiting for transfers between devices: 164 us -> 91.3 us
  starting transfers between devices: 0.09 us -> 11.4 us
    all_gather x1 -> x0, waiting for transfers between devices: 80.9 us -> none  [body(): lax.all_gather(slice_fac, 'blk', axis=0, tiled=True)]
    all_to_all x0 -> x1, waiting for transfers between devices: none -> 52.5 us  [swapped_in(): shards = lax.all_to_all(shards, name, split_axis=0, concat_axis=0)]
    all_gather x1, waiting for transfers between devices: 45.3 us -> 0.6 us  [body(): lax.all_gather(slice_feat, 'blk', axis=0, tiled=True)]
    all_to_all x0 -> x1, starting transfers between devices: none -> 11.4 us  [swapped_in(): shards = lax.all_to_all(shards, name, split_axis=0, concat_axis=0)]
  transfers between devices with their start and end apart: 3 -> 3, of which waited for: 3 -> 3; matrix products, arithmetic and copies ran while one was open for 13% -> 17% of each run, Pallas kernels for 0% -> 0%
where the time goes in v1:
time: 213 us; the launch traced here: 212 us
  waiting for transfers between devices  91.3 us (43%)
  matrix products  88.8 us (42%)
  between operations  13.5 us (6%)
  starting transfers between devices  11.4 us (5%)
  local copies, waits for them, and re-layouts  3.99 us (2%)
  other arithmetic  3.45 us (2%)
    all_to_all x1, waiting for transfers between devices, swapped_in(): shards = lax.all_to_all(shards, name, split_axis=0, concat_axis=0)  52.5 us
    reduce_scatter x1, waiting for transfers between devices, body(): summed = lax.psum_scatter(own_term, 'rep', scatter_dimension=0, tiled=True)  38.2 us
    dot_general x1, matrix products, pair_terms(): jnp.dot(weight, part_feat, precision=hi)  29.5 us
    dot_general x1, matrix products, pair_terms(): cross = jnp.dot(own_feat, part_feat.T, precision=hi)  25.8 us
    dot_general x1, matrix products, pair_terms(): jnp.dot(own_fac[:, rank:], part_fac[:, :rank].T, precision=hi)  17.3 us
    dot_general x1, matrix products, pair_terms(): coupling = jnp.dot(own_fac[:, :rank], part_fac[:, rank:].T, precision=hi)  16.1 us
    all_to_all x1, starting transfers between devices, swapped_in(): shards = lax.all_to_all(shards, name, split_axis=0, concat_axis=0)  11.4 us
  transfers between devices with their start and end apart: 3, of which 3 were waited for; matrix products, arithmetic and copies ran while one was open for 17% of the time, Pallas kernels for 0%

profile of v1, /device:TPU:32, one launch (start us, length us, event | category | flops | bytes accessed | tf_op | source)
XLA Modules:
  0.0 212.4 jit_solution(6651676999008498699)
XLA Ops:
  6.5 0.0 copy-start.2
  6.5 0.9 constant_dynamic-slice_fusion.1
  7.5 1.6 stack.2
  9.0 11.4 %all-to-all-start = ((f32[32,128,128]{2,1,0:T(8,128)}), f32[32,128,128]{2,1,0:T(8,128)S(1)}, u32[]{:S(2)}, u32[]{:S(2)}) async-start(f32[32,128,128]{2,1,0:T(8,128)} %stack.2), calls=%async_computation | async-start | bytes 4194304 | tf_op jit(solution)/shard_map/all_to_all | solution.py:10
  20.4 0.0 all-gather.2.cloned.1.call-start
  20.4 1.5 constant_dynamic-slice_fusion
  21.9 0.0 all-gather.2.cloned.1.call-update
  22.0 0.0 reduce-scatter.2.cloned.1.call-start
  22.0 1.2 multiply_reduce_fusion.1
  23.3 52.5 %all-to-all-done = f32[32,128,128]{2,1,0:T(8,128)S(1)} async-done(((f32[32,128,128]{2,1,0:T(8,128)}), f32[32,128,128]{2,1,0:T(8,128)S(1)}, u32[]{:S(2)}, u32[]{:S(2)}) %all-to-all-start) | async-done | bytes 2097184 | tf_op jit(solution)/shard_map/all_to_all | solution.py:10
  75.8 0.0 copy-start.1
  75.8 17.3 %fusion.4 = f32[4096,1024]{1,0:T(8,128)} fusion(f32[4096,128]{1,0:T(8,128)S(1)} %bitcast.17, f32[1024,128]{1,0:T(8,128)} %param.3), kind=kOutput, calls=%fused_computation.5 | convolution fusion | flops 3221225472 | bytes 19398656 | tf_op jit(solution)/shard_map/dot_general | solution.py:23
  93.1 0.0 copy-done.2
  93.1 16.1 %fusion.6 = f32[4096,1024]{1,0:T(8,128)} fusion(f32[4096,128]{1,0:T(8,128)S(1)} %bitcast.18, f32[1024,128]{1,0:T(8,128)S(1)} %copy-done.2), kind=kOutput, calls=%fused_computation.7 | convolution fusion | flops 3221225472 | bytes 19398656 | tf_op jit(solution)/shard_map/dot_general | solution.py:22
  109.2 0.6 all-gather.2.cloned.1.call-done
  109.8 2.2 %multiply_reduce_fusion = f32[4096]{0:T(1024)S(1)} fusion(f32[4096,128]{1,0:T(8,128)} %all-gather.2.cloned.1.call-done), kind=kLoop, calls=%fused_computation.9 | loop fusion | flops 1044480 | bytes 2113536 | tf_op jit(solution)/shard_map/reduce_sum | solution.py:20
  112.0 0.0 copy-done.1
  112.0 0.0 copy-start
  112.1 25.8 %fusion.12 = (f32[1024]{0:T(1024)S(1)}, f32[1024,4096]{0,1:T(8,128)}) fusion(f32[4096,128]{1,0:T(8,128)} %all-gather.2.cloned.1.call-done, f32[1024,128]{1,0:T(8,128)S(1)} %copy-done.1, f32[4096]{0:T(1024)S(1)} %multiply_reduce_fusion, f32[1024]{0:T(1024)S(1)} %multiply_reduce_fusion.1, f32[4096,1024]{1,0:T(8,128)} %fusion.6, f32[4096,1024]{1,0:T(8,128)} %fusion.4), kind=kOutput, calls=%fused_computation.18 | convolution fusion | flops 6476004352 | bytes 52977664 | tf_op jit(solution)/shard_map/dot_general | solution.py:18
  137.9 0.0 copy-done
  137.9 29.5 %fusion.9 = f32[1024,128]{1,0:T(8,128)} fusion(f32[1024,4096]{0,1:T(8,128)} %get-tuple-element.6, f32[4096,128]{1,0:T(8,128)S(1)} %copy-done, f32[1024,128]{1,0:T(8,128)S(1)} %copy-done.1, f32[1024]{0:T(1024)S(1)} %get-tuple-element.5), kind=kOutput, calls=%fused_computation.12 | convolution fusion | flops 6442975232 | bytes 19927040 | tf_op jit(solution)/shard_map/dot_general | solution.py:25
  167.4 0.0 reduce-scatter.2.cloned.1.call-update
  167.4 38.2 %reduce-scatter.2.cloned.1.call-done = f32[128,128]{1,0:T(8,128)} async-done(((f32[1024,128]{1,0:T(8,128)}), f32[128,128]{1,0:T(8,128)}) %reduce-scatter.2.cloned.1.call-update) | async-done | bytes 65552 | tf_op jit(solution)/shard_map/reduce_scatter | solution.py:44
Async XLA Ops:
  6.5 86.6 %copy-start.2 = (f32[1024,128]{1,0:T(8,128)S(1)}, f32[1024,128]{1,0:T(8,128)}, u32[]{:S(2)}) copy-start(f32[1024,128]{1,0:T(8,128)} %param.3) | copy-start | bytes 1572868
  9.0 66.8 %all-to-all-start = ((f32[32,128,128]{2,1,0:T(8,128)}), f32[32,128,128]{2,1,0:T(8,128)S(1)}, u32[]{:S(2)}, u32[]{:S(2)}) async-start(f32[32,128,128]{2,1,0:T(8,128)} %stack.2), calls=%async_computation | async-start | bytes 4194304 | tf_op jit(solution)/shard_map/all_to_all | solution.py:10
  20.4 89.4 %all-gather.2.cloned.1.call-start = ((), (), s32[]{:S(2)}) async-start(), calls=%async_computation.2 | async-start | bytes 2162688 | tf_op jit(solution)/shard_map/all_gather | solution.py:41
  22.0 183.6 %reduce-scatter.2.cloned.1.call-start = ((), (), s32[]{:S(2)}) async-start(), calls=%async_computation.3 | async-start | bytes 589824 | tf_op jit(solution)/shard_map/reduce_scatter | solution.py:44
  75.8 36.2 %copy-start.1 = (f32[1024,128]{1,0:T(8,128)S(1)}, f32[1024,128]{1,0:T(8,128)}, u32[]{:S(2)}) copy-start(f32[1024,128]{1,0:T(8,128)} %param.2) | copy-start | bytes 1572868
  112.0 25.8 %copy-start = (f32[4096,128]{1,0:T(8,128)S(1)}, f32[4096,128]{1,0:T(8,128)}, u32[]{:S(2)}) copy-start(f32[4096,128]{1,0:T(8,128)} %all-gather.2.cloned.1.call-done) | copy-start | bytes 6291460
Sparse Core Ops, SparseCore 0:
  24.0 85.7 all-gather.1
  167.5 38.0 reduce-scatter.1
